TPU v7x, 32 devices: a whole 2x2x4 slice. The times are simulated.
32 devices in a mesh: dp: 8 (over y, x, core), tensor: 4 (over z).
Axes of the slice: x: 2, y: 2, z: 4, core: 2. Of those that a mesh axis runs over, the one named last changes fastest.
Arguments:
- tokens: bfloat16 [6144, 2048], P(('dp', 'tensor')), may hold values from -6 to 6
- cotangent: bfloat16 [6144, 2048], P(('dp', 'tensor')), may hold values from -6 to 6
- deal: int32 [6144], P(('dp', 'tensor')), may hold values from 0 to 6143, as said below
- segment: int32 [6144], P('dp'), may hold values from 0 to 3, as said below
- norm1_gain: float32 [2, 2048], replicated, may hold values from 0.5 to 1.5
- norm1_shift: float32 [2, 2048], replicated, may hold values from -1.25 to 1.25
- query_weight: bfloat16 [2, 2048, 2048], P(None, 'dp', 'tensor'), may hold values from -0.125 to 0.125
- query_bias: float32 [2, 2048], P(None, 'tensor'), may hold values from -3 to 3
- kv_weight: bfloat16 [2, 2048, 256], P(None, 'dp', 'tensor'), may hold values from -0.125 to 0.125
- value_bias: float32 [2, 128], replicated, may hold values from -0.3125 to 0.3125
- out_weight: bfloat16 [2, 2048, 2048], P(None, 'tensor', 'dp'), may hold values from -1.5 to 1.5
- out_bias: float32 [2, 2048], replicated, may hold values from -1.75 to 1.75
- norm2_gain: float32 [2, 2048], replicated, may hold values from 0.5 to 1.5
- norm2_shift: float32 [2, 2048], replicated, may hold values from -1.25 to 1.25
- up_weight: bfloat16 [2, 2048, 8192], P(None, 'dp', 'tensor'), may hold values from -0.125 to 0.125
- up_bias: float32 [2, 8192], P(None, 'tensor'), may hold values from -3 to 3
- down_weight: bfloat16 [2, 8192, 2048], P(None, 'tensor', 'dp'), may hold values from -0.0625 to 0.0625
- down_bias: float32 [2, 2048], replicated, may hold values from -1.75 to 1.75
Outputs:
- layer_out: bfloat16 [6144, 2048], P(('dp', 'tensor'))
- tokens_grad: bfloat16 [6144, 2048], P(('dp', 'tensor'))
- norm1_gain_grad: float32 [2, 2048], replicated
- norm1_shift_grad: float32 [2, 2048], replicated
- query_weight_grad: float32 [2, 2048, 2048], P(None, 'dp', 'tensor')
- query_bias_grad: float32 [2, 2048], P(None, 'tensor')
- kv_weight_grad: float32 [2, 2048, 256], P(None, 'dp', 'tensor')
- value_bias_grad: float32 [2, 128], replicated
- out_weight_grad: float32 [2, 2048, 2048], P(None, 'tensor', 'dp')
- out_bias_grad: float32 [2, 2048], replicated
- norm2_gain_grad: float32 [2, 2048], replicated
- norm2_shift_grad: float32 [2, 2048], replicated
- up_weight_grad: float32 [2, 2048, 8192], P(None, 'dp', 'tensor')
- up_bias_grad: float32 [2, 8192], P(None, 'tensor')
- down_weight_grad: float32 [2, 8192, 2048], P(None, 'tensor', 'dp')
- down_bias_grad: float32 [2, 2048], replicated
Inputs may be any that keep to these rules, and one draw needn't show every extreme that they name: deal is a permutation: input row i becomes working row deal[i]; rows of both orders are laid out over the devices in order, 192 a device; a row stays on a device of the same tensor index, and every device deals exactly 24 rows to each dp index. `segment`: within each group of 768 working rows the labels never fall; each run of equal labels is one sequence of 96 to 768 rows; the first group is one sequence of all its rows.
All inputs are finite; a program needn't handle non-finite values.
Results may differ from a plain program's by a relative error of at most 0.025.
Values may be sent and summed in bfloat16 or wider, within the bound.
No kernel may reach another device: no remote copies, remote signals or barrier semaphores. Data moves between devices by JAX's collectives and lax.ppermute only.
A program may use at most 256 MiB of HBM per device.

v0:
```python
import jax
import jax.numpy as jnp
from jax import lax
from jax.sharding import PartitionSpec as P

HEAD = 128
EPSILON = 1e-05


def layer_norm(values, scales, offsets):
    row_mean = jnp.mean(values, axis=-1, keepdims=True)
    centred = values - row_mean
    row_var = jnp.mean(centred * centred, axis=-1, keepdims=True)
    return centred * lax.rsqrt(row_var + EPSILON) * scales + offsets


def gelu_tanh(values):
    return jax.nn.gelu(values, approximate=True)


def matmul(left, right):
    return jnp.dot(left, right, preferred_element_type=jnp.float32)


def contract_rows(left, right):
    return lax.dot_general(
        left, right, (((0,), (0,)), ((), ())), preferred_element_type=jnp.float32
    )


def contract_cols(left, right):
    return lax.dot_general(
        left, right, (((1,), (1,)), ((), ())), preferred_element_type=jnp.float32
    )


def rows_gather(values):
    return lax.all_gather(values, "tensor", axis=0, tiled=True)


def grad_gather(values):
    return lax.all_gather(values, "tensor", axis=0, tiled=True)


def rows_scatter(left, right):
    return lax.psum_scatter(
        matmul(left, right).astype(jnp.bfloat16), "tensor", scatter_dimension=0, tiled=True
    ).astype(jnp.float32)


def grad_scatter(factor_pairs):
    running = None
    for gradient, weight in factor_pairs:
        product_piece = contract_cols(gradient, weight)
        running = product_piece if running is None else running + product_piece
    return lax.psum_scatter(
        running.astype(jnp.bfloat16), "tensor", scatter_dimension=0, tiled=True
    ).astype(jnp.float32)


def place_slice(values, full_width, tensor_rank):
    start_col = tensor_rank * values.shape[0]
    return lax.dynamic_update_slice(jnp.zeros((full_width,), jnp.float32), values, (start_col,))


def local(
    tokens,
    cotangent,
    deal,
    segment,
    norm1_gain,
    norm1_shift,
    query_weight,
    query_bias,
    kv_weight,
    value_bias,
    out_weight,
    out_bias,
    norm2_gain,
    norm2_shift,
    up_weight,
    up_bias,
    down_weight,
    down_bias,
):
    local_rows = tokens.shape[0]
    dp_count = lax.axis_size("dp")
    tensor_count = lax.axis_size("tensor")
    tensor_rank = lax.axis_index("tensor")
    slot_rows = local_rows // dp_count
    layer_total = query_weight.shape[0]
    group_rows = local_rows * tensor_count
    query_cols = query_weight.shape[2]
    pair_width = kv_weight.shape[2]
    hidden_cols = up_weight.shape[2]
    head_count = query_cols // HEAD
    score_scale = HEAD ** (-0.5)
    target_dev = deal // local_rows // tensor_count
    target_row = deal % local_rows
    dev_ids = jnp.arange(dp_count, dtype=jnp.int32)
    dev_match = (target_dev[:, None] == dev_ids[None, :]).astype(jnp.int32)
    earlier = jnp.cumsum(dev_match, axis=0) - dev_match
    slot_of = target_dev * slot_rows + jnp.sum(earlier * dev_match, axis=1)
    row_ids = jnp.arange(local_rows, dtype=jnp.int32)
    send_mask = row_ids[:, None] == slot_of[None, :]
    send_table = send_mask.astype(jnp.bfloat16)
    sent_place = jnp.sum(jnp.where(send_mask, target_row[None, :], 0), axis=1)
    arrived_place = lax.all_to_all(sent_place, "dp", split_axis=0, concat_axis=0, tiled=True)
    tokens_sent = matmul(send_table, tokens).astype(jnp.bfloat16)
    tangent_sent = matmul(send_table, cotangent).astype(jnp.bfloat16)
    tokens_come, tangent_come = (
        lax.all_to_all(tokens_sent, "dp", split_axis=0, concat_axis=0, tiled=True),
        lax.all_to_all(tangent_sent, "dp", split_axis=0, concat_axis=0, tiled=True),
    )
    place_table = (row_ids[:, None] == arrived_place[None, :]).astype(jnp.bfloat16)
    stream = matmul(place_table, tokens_come)
    tangent = matmul(place_table, tangent_come)
    places = jnp.arange(group_rows, dtype=jnp.int32)
    allowed = (places[None, :] <= places[:, None]) & (segment[:, None] == segment[None, :])
    saved = []
    kept_weights = []
    for layer_index in range(layer_total):
        w_query, w_pair, w_out, w_up, w_down = (
            lax.all_gather(query_weight[layer_index], "dp", axis=0, tiled=True),
            lax.all_gather(kv_weight[layer_index], "dp", axis=0, tiled=True),
            lax.all_gather(out_weight[layer_index], "dp", axis=1, tiled=True),
            lax.all_gather(up_weight[layer_index], "dp", axis=0, tiled=True),
            lax.all_gather(down_weight[layer_index], "dp", axis=1, tiled=True),
        )
        kept_weights.append(None)
        normed_one = layer_norm(stream, norm1_gain[layer_index], norm1_shift[layer_index]).astype(
            jnp.bfloat16
        )
        normed_all = rows_gather(normed_one)
        queries = (matmul(normed_all, w_query) + query_bias[layer_index]).astype(jnp.bfloat16)
        full_bias = jnp.concatenate([jnp.zeros((HEAD,), jnp.float32), value_bias[layer_index]])
        pair_bias = lax.dynamic_slice_in_dim(full_bias, tensor_rank * pair_width, pair_width)
        pair_local = (matmul(normed_all, w_pair) + pair_bias).astype(jnp.bfloat16)
        pair_all = lax.all_gather(pair_local, "tensor", axis=1, tiled=True)
        key_rows = pair_all[:, :HEAD]
        value_rows = pair_all[:, HEAD:]
        query_heads = jnp.transpose(queries.reshape(group_rows, head_count, HEAD), (1, 0, 2))

        def attend(query_one):
            scores = jnp.where(allowed, contract_cols(query_one, key_rows) * score_scale, -1e30)
            row_top = jnp.max(scores, axis=-1, keepdims=True)
            exp_score = jnp.exp(scores - row_top)
            row_total = jnp.sum(exp_score, axis=-1, keepdims=True)
            weights = (exp_score / row_total).astype(jnp.bfloat16)
            return (matmul(weights, value_rows), (row_top + jnp.log(row_total))[:, 0])

        head_outs, log_totals = lax.map(attend, query_heads)
        mixed = (
            jnp.transpose(head_outs, (1, 0, 2)).reshape(group_rows, query_cols).astype(jnp.bfloat16)
        )
        hidden_state = stream + rows_scatter(mixed, w_out) + out_bias[layer_index]
        normed_two = layer_norm(
            hidden_state, norm2_gain[layer_index], norm2_shift[layer_index]
        ).astype(jnp.bfloat16)
        normed_two_all = rows_gather(normed_two)
        pre_gelu = matmul(normed_two_all, w_up) + up_bias[layer_index]
        activation = gelu_tanh(pre_gelu).astype(jnp.bfloat16)
        saved.append(
            (
                stream,
                normed_all,
                queries,
                pair_all,
                log_totals,
                mixed,
                hidden_state,
                normed_two_all,
                pre_gelu,
                activation,
            )
        )
        stream = hidden_state + rows_scatter(activation, w_down) + down_bias[layer_index]
    layer_out = stream.astype(jnp.bfloat16)
    reduced_by_layer = [None] * layer_total
    small_by_layer = [None] * layer_total
    for layer_index in reversed(range(layer_total)):
        (
            stream_in,
            normed_all,
            queries,
            pair_all,
            log_totals,
            mixed,
            hidden_state,
            normed_two_all,
            pre_gelu,
            activation,
        ) = saved[layer_index]
        w_query, w_pair, w_out, w_up, w_down = (
            lax.all_gather(query_weight[layer_index], "dp", axis=0, tiled=True),
            lax.all_gather(kv_weight[layer_index], "dp", axis=0, tiled=True),
            lax.all_gather(out_weight[layer_index], "dp", axis=1, tiled=True),
            lax.all_gather(up_weight[layer_index], "dp", axis=0, tiled=True),
            lax.all_gather(down_weight[layer_index], "dp", axis=1, tiled=True),
        )
        key_rows = pair_all[:, :HEAD]
        value_rows = pair_all[:, HEAD:]
        branch_grad = tangent.astype(jnp.bfloat16)
        down_bias_part = jnp.sum(branch_grad.astype(jnp.float32), axis=0)
        branch_all = grad_gather(branch_grad)
        down_grad = contract_rows(activation, branch_all)
        act_grad = contract_cols(branch_all, w_down)
        pre_grad = jax.vjp(gelu_tanh, pre_gelu)[1](act_grad)[0].astype(jnp.bfloat16)
        up_bias_part = jnp.sum(pre_grad.astype(jnp.float32), axis=0)
        up_grad = contract_rows(normed_two_all, pre_grad)
        normed_two_grad = grad_scatter(((pre_grad, w_up),))
        norm_pull_two = jax.vjp(
            layer_norm, hidden_state, norm2_gain[layer_index], norm2_shift[layer_index]
        )[1]
        hidden_part, gain_two_part, shift_two_part = norm_pull_two(normed_two_grad)
        hidden_grad = tangent + hidden_part
        attn_grad = hidden_grad.astype(jnp.bfloat16)
        out_bias_part = jnp.sum(attn_grad.astype(jnp.float32), axis=0)
        attn_all = grad_gather(attn_grad)
        out_grad = contract_rows(mixed, attn_all)
        mixed_grad = contract_cols(attn_all, w_out).astype(jnp.bfloat16)
        query_heads = jnp.transpose(queries.reshape(group_rows, head_count, HEAD), (1, 0, 2))
        dout_heads = jnp.transpose(mixed_grad.reshape(group_rows, head_count, HEAD), (1, 0, 2))

        def attend_back(carried, inputs):
            query_one, dout_one, log_one = inputs
            scores = jnp.where(allowed, contract_cols(query_one, key_rows) * score_scale, -1e30)
            probs = jnp.exp(scores - log_one[:, None])
            prob_grad = contract_cols(dout_one, value_rows)
            inner = jnp.sum(probs * prob_grad, axis=-1, keepdims=True)
            score_grad = (probs * (prob_grad - inner) * score_scale).astype(jnp.bfloat16)
            key_acc = carried[0] + contract_rows(score_grad, query_one)
            value_acc = carried[1] + contract_rows(probs.astype(jnp.bfloat16), dout_one)
            return ((key_acc, value_acc), matmul(score_grad, key_rows))

        start_acc = (
            jnp.zeros((group_rows, HEAD), jnp.float32),
            jnp.zeros((group_rows, HEAD), jnp.float32),
        )
        (key_grad, value_grad), query_grads = lax.scan(
            attend_back, start_acc, (query_heads, dout_heads, log_totals)
        )
        query_grad = (
            jnp.transpose(query_grads, (1, 0, 2))
            .reshape(group_rows, query_cols)
            .astype(jnp.bfloat16)
        )
        query_bias_part = jnp.sum(query_grad.astype(jnp.float32), axis=0)
        pair_part = jnp.concatenate([key_grad, value_grad], axis=1)
        pair_grad = lax.psum_scatter(
            pair_part.astype(jnp.bfloat16), "tensor", scatter_dimension=1, tiled=True
        )
        pair_bias_part = jnp.sum(pair_grad.astype(jnp.float32), axis=0)
        query_w_grad = contract_rows(normed_all, query_grad)
        pair_w_grad = contract_rows(normed_all, pair_grad)
        normed_grad = grad_scatter(((query_grad, w_query), (pair_grad, w_pair)))
        norm_pull_one = jax.vjp(
            layer_norm, stream_in, norm1_gain[layer_index], norm1_shift[layer_index]
        )[1]
        stream_part, gain_one_part, shift_one_part = norm_pull_one(normed_grad)
        tangent = hidden_grad + stream_part
        small_by_layer[layer_index] = (
            gain_one_part,
            shift_one_part,
            place_slice(query_bias_part, query_cols * tensor_count, tensor_rank),
            place_slice(pair_bias_part, pair_width * tensor_count, tensor_rank),
            out_bias_part,
            gain_two_part,
            shift_two_part,
            place_slice(up_bias_part, hidden_cols * tensor_count, tensor_rank),
            down_bias_part,
        )
        reduced_by_layer[layer_index] = (
            lax.psum_scatter(
                query_w_grad.astype(jnp.bfloat16), "dp", scatter_dimension=0, tiled=True
            ).astype(jnp.float32),
            lax.psum_scatter(
                pair_w_grad.astype(jnp.bfloat16), "dp", scatter_dimension=0, tiled=True
            ).astype(jnp.float32),
            lax.psum_scatter(
                out_grad.astype(jnp.bfloat16), "dp", scatter_dimension=1, tiled=True
            ).astype(jnp.float32),
            lax.psum_scatter(
                up_grad.astype(jnp.bfloat16), "dp", scatter_dimension=0, tiled=True
            ).astype(jnp.float32),
            lax.psum_scatter(
                down_grad.astype(jnp.bfloat16), "dp", scatter_dimension=1, tiled=True
            ).astype(jnp.float32),
        )
    summed = [
        jnp.stack([reduced_by_layer[layer_index][member] for layer_index in range(layer_total)])
        for member in range(5)
    ]
    smalls = [
        jnp.stack([small_by_layer[layer_index][member] for layer_index in range(layer_total)])
        for member in range(9)
    ]
    (
        gain_one_sum,
        shift_one_sum,
        query_bias_sum,
        pair_bias_sum,
        out_bias_sum,
        gain_two_sum,
        shift_two_sum,
        up_bias_sum,
        down_bias_sum,
    ) = lax.psum(
        (
            smalls[0],
            smalls[1],
            smalls[2],
            smalls[3],
            smalls[4],
            smalls[5],
            smalls[6],
            smalls[7],
            smalls[8],
        ),
        ("dp", "tensor"),
    )
    query_bias_grad = lax.dynamic_slice_in_dim(
        query_bias_sum, tensor_rank * query_cols, query_cols, 1
    )
    up_bias_grad = lax.dynamic_slice_in_dim(up_bias_sum, tensor_rank * hidden_cols, hidden_cols, 1)
    value_bias_grad = pair_bias_sum[:, HEAD:]
    out_slots = contract_rows(place_table, layer_out).astype(jnp.bfloat16)
    grad_slots = contract_rows(place_table, tangent.astype(jnp.bfloat16)).astype(jnp.bfloat16)
    out_back, grad_back = (
        lax.all_to_all(out_slots, "dp", split_axis=0, concat_axis=0, tiled=True),
        lax.all_to_all(grad_slots, "dp", split_axis=0, concat_axis=0, tiled=True),
    )
    layer_rows = contract_rows(send_table, out_back).astype(jnp.bfloat16)
    token_rows = contract_rows(send_table, grad_back).astype(jnp.bfloat16)
    return (
        layer_rows,
        token_rows,
        gain_one_sum,
        shift_one_sum,
        summed[0],
        query_bias_grad,
        summed[1],
        value_bias_grad,
        summed[2],
        out_bias_sum,
        gain_two_sum,
        shift_two_sum,
        summed[3],
        up_bias_grad,
        summed[4],
        down_bias_sum,
    )


def solution(mesh):
    in_specs = (
        P(("dp", "tensor"), None),
        P(("dp", "tensor"), None),
        P(("dp", "tensor")),
        P("dp"),
        P(),
        P(),
        P(None, "dp", "tensor"),
        P(None, "tensor"),
        P(None, "dp", "tensor"),
        P(),
        P(None, "tensor", "dp"),
        P(),
        P(),
        P(),
        P(None, "dp", "tensor"),
        P(None, "tensor"),
        P(None, "tensor", "dp"),
        P(),
    )
    out_specs = (
        P(("dp", "tensor"), None),
        P(("dp", "tensor"), None),
        P(),
        P(),
        P(None, "dp", "tensor"),
        P(None, "tensor"),
        P(None, "dp", "tensor"),
        P(),
        P(None, "tensor", "dp"),
        P(),
        P(),
        P(),
        P(None, "dp", "tensor"),
        P(None, "tensor"),
        P(None, "tensor", "dp"),
        P(),
    )
    return jax.shard_map(local, mesh=mesh, in_specs=in_specs, out_specs=out_specs, check_vma=False)
```

profile of v0, /device:TPU:0, one launch (start us, length us, event | category | flops | bytes accessed | tf_op | source)
XLA Modules:
  0.0 2494.6 jit_solution(4482688082752972419)
XLA Ops:
  50.9 50.5 %all-gather.27.cloned.1.call-done = bf16[768,2048]{1,0:T(8,128)(2,1)} async-done(((bf16[192,2048]{1,0:T(8,128)(2,1)}), bf16[768,2048]{1,0:T(8,128)(2,1)}) %all-gather.27.cloned.1.call-update) | async-done | bytes 3145744 | tf_op jit(solution)/shard_map/all_gather | solution.py:38
  179.2 56.9 %reduce-scatter.25.cloned.1.call-done = bf16[192,2048]{1,0:T(8,128)(2,1)} async-done(((bf16[768,2048]{1,0:T(8,128)(2,1)}), bf16[192,2048]{1,0:T(8,128)(2,1)}) %reduce-scatter.25.cloned.1.call-update) | async-done | bytes 786448 | tf_op jit(solution)/shard_map/reduce_scatter | solution.py:46
  242.8 50.0 %all-gather.47.cloned.1.call-done = bf16[1,2048,2048]{2,1,0:T(8,128)(2,1)} async-done(((bf16[1,256,2048]{2,1,0:T(8,128)(2,1)}), bf16[1,2048,2048]{2,1,0:T(8,128)(2,1)}) %all-gather.47.cloned.1.call-update) | async-done | bytes 8388624 | tf_op jit(solution)/shard_map/all_gather | solution.py:127
  292.9 65.5 %all-gather.29.cloned.1.call-done = bf16[768,2048]{1,0:T(8,128)(2,1)} async-done(((bf16[192,2048]{1,0:T(8,128)(2,1)}), bf16[768,2048]{1,0:T(8,128)(2,1)}) %all-gather.29.cloned.1.call-update) | async-done | bytes 3145744 | tf_op jit(solution)/shard_map/all_gather | solution.py:38
  370.1 45.4 %all-gather.49.cloned.1.call-done = bf16[1,2048,2048]{2,1,0:T(8,128)(2,1)} async-done(((bf16[1,2048,256]{2,1,0:T(8,128)(2,1)}), bf16[1,2048,2048]{2,1,0:T(8,128)(2,1)}) %all-gather.49.cloned.1.call-update) | async-done | bytes 8388624 | tf_op jit(solution)/shard_map/all_gather | solution.py:128
  430.0 59.0 %reduce-scatter.27.cloned.1.call-done = bf16[192,2048]{1,0:T(8,128)(2,1)} async-done(((bf16[768,2048]{1,0:T(8,128)(2,1)}), bf16[192,2048]{1,0:T(8,128)(2,1)}) %reduce-scatter.27.cloned.1.call-update) | async-done | bytes 786448 | tf_op jit(solution)/shard_map/reduce_scatter | solution.py:46
  518.9 65.5 %all-gather.31.cloned.1.call-done = bf16[768,2048]{1,0:T(8,128)(2,1)} async-done(((bf16[192,2048]{1,0:T(8,128)(2,1)}), bf16[768,2048]{1,0:T(8,128)(2,1)}) %all-gather.31.cloned.1.call-update) | async-done | bytes 3145744 | tf_op jit(solution)/shard_map/all_gather | solution.py:38
  651.2 57.8 %reduce-scatter.29.cloned.1.call-done = bf16[192,2048]{1,0:T(8,128)(2,1)} async-done(((bf16[768,2048]{1,0:T(8,128)(2,1)}), bf16[192,2048]{1,0:T(8,128)(2,1)}) %reduce-scatter.29.cloned.1.call-update) | async-done | bytes 786448 | tf_op jit(solution)/shard_map/reduce_scatter | solution.py:46
  770.2 65.5 %all-gather.33.cloned.1.call-done = bf16[768,2048]{1,0:T(8,128)(2,1)} async-done(((bf16[192,2048]{1,0:T(8,128)(2,1)}), bf16[768,2048]{1,0:T(8,128)(2,1)}) %all-gather.33.cloned.1.call-update) | async-done | bytes 3145744 | tf_op jit(solution)/shard_map/all_gather | solution.py:38
  847.5 52.4 %all-gather.35.cloned.1.call-done = bf16[768,2048]{1,0:T(8,128)(2,1)} async-done(((bf16[192,2048]{1,0:T(8,128)(2,1)}), bf16[768,2048]{1,0:T(8,128)(2,1)}) %all-gather.35.cloned.1.call-update) | async-done | bytes 3145744 | tf_op jit(solution)/shard_map/all_gather | solution.py:42
  899.9 56.9 %all-gather.57.cloned.1.call-done = bf16[1,2048,2048]{2,1,0:T(8,128)(2,1)} async-done(((bf16[1,2048,256]{2,1,0:T(8,128)(2,1)}), bf16[1,2048,2048]{2,1,0:T(8,128)(2,1)}) %all-gather.57.cloned.1.call-update) | async-done | bytes 8388624 | tf_op jit(solution)/shard_map/all_gather | solution.py:128
  982.1 60.4 %reduce-scatter.33.cloned.1.call-done = bf16[192,2048]{1,0:T(8,128)(2,1)} async-done(((bf16[768,2048]{1,0:T(8,128)(2,1)}), bf16[192,2048]{1,0:T(8,128)(2,1)}) %reduce-scatter.33.cloned.1.call-update) | async-done | bytes 786448 | tf_op jit(solution)/shard_map/reduce_scatter | solution.py:56
  1047.8 63.4 %all-gather.37.cloned.1.call-done = bf16[768,2048]{1,0:T(8,128)(2,1)} async-done(((bf16[192,2048]{1,0:T(8,128)(2,1)}), bf16[768,2048]{1,0:T(8,128)(2,1)}) %all-gather.37.cloned.1.call-update) | async-done | bytes 3145744 | tf_op jit(solution)/shard_map/all_gather | solution.py:42
  1189.3 58.6 %reduce-scatter.35.cloned.1.call-done = bf16[192,2048]{1,0:T(8,128)(2,1)} async-done(((bf16[768,2048]{1,0:T(8,128)(2,1)}), bf16[192,2048]{1,0:T(8,128)(2,1)}) %reduce-scatter.35.cloned.1.call-update) | async-done | bytes 786448 | tf_op jit(solution)/shard_map/reduce_scatter | solution.py:56
  1256.2 63.2 %all-gather.39.cloned.1.call-done = bf16[768,2048]{1,0:T(8,128)(2,1)} async-done(((bf16[192,2048]{1,0:T(8,128)(2,1)}), bf16[768,2048]{1,0:T(8,128)(2,1)}) %all-gather.39.cloned.1.call-update) | async-done | bytes 3145744 | tf_op jit(solution)/shard_map/all_gather | solution.py:42
  1346.1 59.0 %reduce-scatter.37.cloned.1.call-done = bf16[192,2048]{1,0:T(8,128)(2,1)} async-done(((bf16[768,2048]{1,0:T(8,128)(2,1)}), bf16[192,2048]{1,0:T(8,128)(2,1)}) %reduce-scatter.37.cloned.1.call-update) | async-done | bytes 786448 | tf_op jit(solution)/shard_map/reduce_scatter | solution.py:56
  1411.3 63.4 %all-gather.41.cloned.1.call-done = bf16[768,2048]{1,0:T(8,128)(2,1)} async-done(((bf16[192,2048]{1,0:T(8,128)(2,1)}), bf16[768,2048]{1,0:T(8,128)(2,1)}) %all-gather.41.cloned.1.call-update) | async-done | bytes 3145744 | tf_op jit(solution)/shard_map/all_gather | solution.py:42
  1647.6 80.4 %all-reduce.7.cloned.1.call-done = f32[2,8192]{1,0:T(2,128)} async-done(((f32[2,8192]{1,0:T(2,128)}), f32[2,8192]{1,0:T(2,128)}) %all-reduce.7.cloned.1.call-update) | async-done | bytes 65552 | tf_op jit(solution)/shard_map/psum | solution.py:308
  1803.6 73.3 %reduce-scatter.59.cloned.1.call-done = bf16[2048,256]{1,0:T(8,128)(2,1)} async-done(((bf16[2048,2048]{1,0:T(8,128)(2,1)}), bf16[2048,256]{1,0:T(8,128)(2,1)}) %reduce-scatter.59.cloned.1.call-update) | async-done | bytes 1048592 | tf_op jit(solution)/shard_map/reduce_scatter | solution.py:286
  1876.9 75.0 %reduce-scatter.57.cloned.1.call-done = bf16[2048,256]{1,0:T(8,128)(2,1)} async-done(((bf16[2048,2048]{1,0:T(8,128)(2,1)}), bf16[2048,256]{1,0:T(8,128)(2,1)}) %reduce-scatter.57.cloned.1.call-update) | async-done | bytes 1048592 | tf_op jit(solution)/shard_map/reduce_scatter | solution.py:286
  1955.9 59.2 %reduce-scatter.39.cloned.1.call-done = bf16[192,2048]{1,0:T(8,128)(2,1)} async-done(((bf16[768,2048]{1,0:T(8,128)(2,1)}), bf16[192,2048]{1,0:T(8,128)(2,1)}) %reduce-scatter.39.cloned.1.call-update) | async-done | bytes 786448 | tf_op jit(solution)/shard_map/reduce_scatter | solution.py:56
  2024.5 65.4 %reduce-scatter.55.cloned.1.call-done = bf16[256,2048]{1,0:T(8,128)(2,1)} async-done(((bf16[2048,2048]{1,0:T(8,128)(2,1)}), bf16[256,2048]{1,0:T(8,128)(2,1)}) %reduce-scatter.55.cloned.1.call-update) | async-done | bytes 1048592 | tf_op jit(solution)/shard_map/reduce_scatter | solution.py:283
  2089.9 75.0 %reduce-scatter.53.cloned.1.call-done = bf16[256,2048]{1,0:T(8,128)(2,1)} async-done(((bf16[2048,2048]{1,0:T(8,128)(2,1)}), bf16[256,2048]{1,0:T(8,128)(2,1)}) %reduce-scatter.53.cloned.1.call-update) | async-done | bytes 1048592 | tf_op jit(solution)/shard_map/reduce_scatter | solution.py:283
  2345.6 130.5 %all-reduce.9.cloned.1.call-done = (f32[2,2048]{1,0:T(2,128)}, f32[2,2048]{1,0:T(2,128)}, f32[2,2048]{1,0:T(2,128)}, f32[2,256]{1,0:T(2,128)}, f32[2,2048]{1,0:T...) async-done(((f32[2,2048]{1,0:T(2,128)}, f32[2,2048]{1,0:T(2,128)}, f32[2,2048]{1,0:T(2,128)}, f32[2,256]{1,0:T(2,128)}, f32[2,2048]{1,0:T(2,128)}, ...) | async-done | bytes 116752 | tf_op jit(solution)/shard_map/psum | solution.py:308
  (656 shorter events, 1077.6 us)
Async XLA Ops:
  40.1 196.0 %reduce-scatter.25.cloned.1.call-start = ((), (), s32[]{:S(2)}) async-start(), calls=%async_computation.26 | async-start | bytes 3932160 | tf_op jit(solution)/shard_map/reduce_scatter | solution.py:46
  179.0 179.4 %all-gather.29.cloned.1.call-start = ((), (), s32[]{:S(2)}) async-start(), calls=%async_computation.27 | async-start | bytes 3932160 | tf_op jit(solution)/shard_map/all_gather | solution.py:38
  239.2 176.3 %all-gather.49.cloned.1.call-start = ((), (), s32[]{:S(2)}) async-start(), calls=%async_computation.55 | async-start | bytes 9437184 | tf_op jit(solution)/shard_map/all_gather | solution.py:128
  242.3 246.7 %reduce-scatter.27.cloned.1.call-start = ((), (), s32[]{:S(2)}) async-start(), calls=%async_computation.28 | async-start | bytes 3932160 | tf_op jit(solution)/shard_map/reduce_scatter | solution.py:46
  429.3 155.0 %all-gather.31.cloned.1.call-start = ((), (), s32[]{:S(2)}) async-start(), calls=%async_computation.29 | async-start | bytes 3932160 | tf_op jit(solution)/shard_map/all_gather | solution.py:38
  492.9 216.2 %reduce-scatter.29.cloned.1.call-start = ((), (), s32[]{:S(2)}) async-start(), calls=%async_computation.30 | async-start | bytes 3932160 | tf_op jit(solution)/shard_map/reduce_scatter | solution.py:46
  651.2 184.6 %all-gather.33.cloned.1.call-start = ((), (), s32[]{:S(2)}) async-start(), calls=%async_computation.31 | async-start | bytes 3932160 | tf_op jit(solution)/shard_map/all_gather | solution.py:38
  712.1 187.8 %all-gather.35.cloned.1.call-start = ((), (), s32[]{:S(2)}) async-start(), calls=%async_computation.33 | async-start | bytes 3932160 | tf_op jit(solution)/shard_map/all_gather | solution.py:42
  737.2 219.7 %all-gather.57.cloned.1.call-start = ((), (), s32[]{:S(2)}) async-start(), calls=%async_computation.59 | async-start | bytes 9437184 | tf_op jit(solution)/shard_map/all_gather | solution.py:128
  737.7 304.7 %reduce-scatter.33.cloned.1.call-start = ((), (), s32[]{:S(2)}) async-start(), calls=%async_computation.34 | async-start | bytes 3932160 | tf_op jit(solution)/shard_map/reduce_scatter | solution.py:56
  1536.7 191.2 %all-reduce.7.cloned.1.call-start = ((), (), s32[]{:S(2)}) async-start(), calls=%async_computation.49 | async-start | bytes 131072 | tf_op jit(solution)/shard_map/psum | solution.py:308
  1538.1 227.1 %reduce-scatter.47.cloned.1.call-start = ((), (), s32[]{:S(2)}) async-start(), calls=%async_computation.44 | async-start | bytes 294912 | tf_op jit(solution)/shard_map/reduce_scatter | solution.py:277
  1541.4 260.8 %reduce-scatter.45.cloned.1.call-start = ((), (), s32[]{:S(2)}) async-start(), calls=%async_computation.43 | async-start | bytes 294912 | tf_op jit(solution)/shard_map/reduce_scatter | solution.py:277
  1545.2 331.8 %reduce-scatter.59.cloned.1.call-start = ((), (), s32[]{:S(2)}) async-start(), calls=%async_computation.51 | async-start | bytes 9437184 | tf_op jit(solution)/shard_map/reduce_scatter | solution.py:286
  1558.0 393.9 %reduce-scatter.57.cloned.1.call-start = ((), (), s32[]{:S(2)}) async-start(), calls=%async_computation.50 | async-start | bytes 9437184 | tf_op jit(solution)/shard_map/reduce_scatter | solution.py:286
  1571.3 443.8 %reduce-scatter.39.cloned.1.call-start = ((), (), s32[]{:S(2)}) async-start(), calls=%async_computation.40 | async-start | bytes 3932160 | tf_op jit(solution)/shard_map/reduce_scatter | solution.py:56
  1578.7 511.2 %reduce-scatter.55.cloned.1.call-start = ((), (), s32[]{:S(2)}) async-start(), calls=%async_computation.48 | async-start | bytes 9437184 | tf_op jit(solution)/shard_map/reduce_scatter | solution.py:283
  1591.5 573.4 %reduce-scatter.53.cloned.1.call-start = ((), (), s32[]{:S(2)}) async-start(), calls=%async_computation.47 | async-start | bytes 9437184 | tf_op jit(solution)/shard_map/reduce_scatter | solution.py:283
  1604.2 605.2 %reduce-scatter.51.cloned.1.call-start = ((), (), s32[]{:S(2)}) async-start(), calls=%async_computation.46 | async-start | bytes 2359296 | tf_op jit(solution)/shard_map/reduce_scatter | solution.py:280
  1610.4 643.9 %reduce-scatter.49.cloned.1.call-start = ((), (), s32[]{:S(2)}) async-start(), calls=%async_computation.45 | async-start | bytes 2359296 | tf_op jit(solution)/shard_map/reduce_scatter | solution.py:280
  1616.0 682.8 %reduce-scatter.43.cloned.1.call-start = ((), (), s32[]{:S(2)}) async-start(), calls=%async_computation.42 | async-start | bytes 2359296 | tf_op jit(solution)/shard_map/reduce_scatter | solution.py:274
  1628.8 714.8 %reduce-scatter.41.cloned.1.call-start = ((), (), s32[]{:S(2)}) async-start(), calls=%async_computation.41 | async-start | bytes 2359296 | tf_op jit(solution)/shard_map/reduce_scatter | solution.py:274
  2020.8 457.8 %all-to-all-start.4 = ((bf16[8,24,2048]{2,1,0:T(8,128)(2,1)}), bf16[8,24,2048]{2,1,0:T(8,128)(2,1)S(1)}, u32[]{:S(2)}, u32[]{:S(2)}) async-start(bf16[8,24,2048]{2,1,0:T(8,128)(2,1)} %bitcast.336), calls=%async_computation.12 | async-start | bytes 1572864 | tf_op jit(solution)/shard_map/all_to_all | solution.py:331
  2024.5 451.7 %all-reduce.9.cloned.1.call-start = ((), (), s32[]{:S(2)}) async-start(), calls=%async_computation.62 | async-start | bytes 233472 | tf_op jit(solution)/shard_map/psum | solution.py:308
  (154 other events, 7218.9 us)
Sparse Core Ops, SparseCore 0:
  38.4 62.8 all-gather.26
  175.9 60.1 reduce-scatter.24
  294.9 63.4 all-gather.28
  428.7 60.2 reduce-scatter.26
  520.9 63.4 all-gather.30
  650.5 58.4 reduce-scatter.28
  710.9 59.2 all-gather.54
  772.2 63.4 all-gather.32
  837.7 62.1 all-gather.34
  902.2 54.5 all-gather.56
  982.1 60.2 reduce-scatter.32
  1047.6 63.5 all-gather.36
  1189.4 58.5 reduce-scatter.34
  1255.8 63.5 all-gather.38
  1346.2 58.8 reduce-scatter.36
  1411.2 63.5 all-gather.40
  1545.7 58.5 reduce-scatter.30
  1610.3 117.5 all-reduce.6
  1805.6 71.2 reduce-scatter.58
  1880.6 71.2 reduce-scatter.56
  1954.8 60.2 reduce-scatter.38
  2018.6 71.2 reduce-scatter.54
  2093.6 71.2 reduce-scatter.52
  2351.1 124.9 all-reduce.8
  (14 shorter events, 489.1 us)
where the time goes:
time: 2510 us; the launch traced here: 2490 us
  waiting for transfers between devices  1890 us (75%)
  matrix products  350 us (14%)
  other arithmetic  79.2 us (3%)
  blocking collectives  72.6 us (3%)
  local copies, waits for them, and re-layouts  65.7 us (3%)
    all_gather x4, waiting for transfers between devices, rows_gather(): return lax.all_gather(values, 'tensor', axis=0, tiled=True)  247 us
    all_gather x4, waiting for transfers between devices, grad_gather(): return lax.all_gather(values, 'tensor', axis=0, tiled=True)  242 us
    reduce_scatter x4, waiting for transfers between devices, grad_scatter(): lax.psum_scatter(running.astype(jnp.bfloat16), 'tensor', scatter_dimensio...  237 us
    psum x2, waiting for transfers between devices, local(): lax.psum((smalls[0], smalls[1], smalls[2], smalls[3], smalls[4], smalls[5...  211 us
    reduce_scatter x4, waiting for transfers between devices, rows_scatter(): lax.psum_scatter(matmul(left, right).astype(jnp.bfloat16), 'tensor', scat...  174 us
    reduce_scatter x2, waiting for transfers between devices, local(): lax.psum_scatter(down_grad.astype(jnp.bfloat16), 'dp', scatter_dimension=...  148 us
    reduce_scatter x2, waiting for transfers between devices, local(): lax.psum_scatter(up_grad.astype(jnp.bfloat16), 'dp', scatter_dimension=0,...  140 us
    dot_general x34, matrix products, contract_cols(): lax.dot_general(left, right, (((1,), (1,)), ((), ())), preferred_element_...  118 us
  transfers between devices with their start and end apart: 42, of which 38 were waited for; matrix products, arithmetic and copies ran while one was open for 11% of the time, Pallas kernels for 0%

commit v1 on v0

--- a/solution.py
+++ b/solution.py
@@ -5,6 +5,19 @@
 
 HEAD = 128
 EPSILON = 1e-05
+
+
+def gather_around(shard, axis, dim):
+    ways = lax.axis_size(axis)
+    up = [(d, (d + 1) % ways) for d in range(ways)]
+    down = [(d, (d - 1) % ways) for d in range(ways)]
+    earlier, later = ([shard], [shard])
+    for _ in range(ways // 2):
+        earlier.append(lax.ppermute(earlier[-1], axis, up))
+    for _ in range((ways - 1) // 2):
+        later.append(lax.ppermute(later[-1], axis, down))
+    line = jnp.concatenate([*earlier[::-1], *later[1:]], axis=dim)
+    return jnp.roll(line, (lax.axis_index(axis) - ways // 2) * shard.shape[dim], axis=dim)
 
 
 def layer_norm(values, scales, offsets):
@@ -35,7 +48,7 @@
 
 
 def rows_gather(values):
-    return lax.all_gather(values, "tensor", axis=0, tiled=True)
+    return gather_around(values, "tensor", 0)
 
 
 def grad_gather(values):

time: 2510 us -> 2340 us (0.932)
  waiting for transfers between devices: 1890 us -> 1610 us
  starting transfers between devices: 20.6 us -> 87.9 us
  other arithmetic: 79.2 us -> 137 us
    all_gather x4 -> x0, waiting for transfers between devices: 247 us -> none  [rows_gather(): return lax.all_gather(values, 'tensor', axis=0, tiled=True)]
    ppermute x0 -> x12, waiting for transfers between devices: none -> 123 us  [the longest x8 120 us: gather_around(): earlier.append(lax.ppermute(earlier[-1], axis, up))]
    all_gather x2, waiting for transfers between devices: 82.3 us -> 0.02 us  [local(): lax.all_gather(up_weight[layer_index], 'dp', axis=0, tiled=True)]
    ppermute x0 -> x12, starting transfers between devices: none -> 70.5 us  [the longest x8 59.7 us: gather_around(): earlier.append(lax.ppermute(earlier[-1], axis, up))]
    concatenate x0 -> x4, other arithmetic: none -> 61.2 us  [gather_around(): jnp.roll(line, (lax.axis_index(axis) - ways // 2) * shard.shape[dim], axi...]
    all_gather x2, waiting for transfers between devices: 25.5 us -> 0.04 us  [local(): lax.all_gather(query_weight[layer_index], 'dp', axis=0, tiled=True)]
  transfers between devices with their start and end apart: 42 -> 50, of which waited for: 38 -> 40; matrix products, arithmetic and copies ran while one was open for 11% -> 14% of each run, Pallas kernels for 0% -> 0%
where the time goes in v1:
time: 2340 us
  waiting for transfers between devices  1610 us (69%)
  matrix products  356 us (15%)
  other arithmetic  137 us (6%)
  starting transfers between devices  87.9 us (4%)
  local copies, waits for them, and re-layouts  67.2 us (3%)
  blocking collectives  64 us (3%)
    reduce_scatter x4, waiting for transfers between devices, grad_scatter(): lax.psum_scatter(running.astype(jnp.bfloat16), 'tensor', scatter_dimensio...  236 us
    all_gather x4, waiting for transfers between devices, grad_gather(): return lax.all_gather(values, 'tensor', axis=0, tiled=True)  228 us
    psum x2, waiting for transfers between devices, local(): lax.psum((smalls[0], smalls[1], smalls[2], smalls[3], smalls[4], smalls[5...  208 us
    reduce_scatter x4, waiting for transfers between devices, rows_scatter(): lax.psum_scatter(matmul(left, right).astype(jnp.bfloat16), 'tensor', scat...  153 us
    reduce_scatter x2, waiting for transfers between devices, local(): lax.psum_scatter(down_grad.astype(jnp.bfloat16), 'dp', scatter_dimension=...  148 us
    reduce_scatter x2, waiting for transfers between devices, local(): lax.psum_scatter(up_grad.astype(jnp.bfloat16), 'dp', scatter_dimension=0,...  141 us
    dot_general x30, matrix products, contract_rows(): lax.dot_general(left, right, (((0,), (0,)), ((), ())), preferred_element_...  121 us
    ppermute x8, waiting for transfers between devices, gather_around(): earlier.append(lax.ppermute(earlier[-1], axis, up))  120 us
  transfers between devices with their start and end apart: 50, of which 40 were waited for; matrix products, arithmetic and copies ran while one was open for 14% of the time, Pallas kernels for 0%

profile of v1, /device:TPU:0, one launch (start us, length us, event | category | flops | bytes accessed | tf_op | source)
XLA Modules:
  0.0 2337.2 jit_solution(8438404686743758265)
XLA Ops:
  178.8 54.7 %reduce-scatter.25.cloned.1.call-done = bf16[192,2048]{1,0:T(8,128)(2,1)} async-done(((bf16[768,2048]{1,0:T(8,128)(2,1)}), bf16[192,2048]{1,0:T(8,128)(2,1)}) %reduce-scatter.25.cloned.1.call-update) | async-done | bytes 786448 | tf_op jit(solution)/shard_map/reduce_scatter | solution.py:59
  363.1 59.0 %reduce-scatter.27.cloned.1.call-done = bf16[192,2048]{1,0:T(8,128)(2,1)} async-done(((bf16[768,2048]{1,0:T(8,128)(2,1)}), bf16[192,2048]{1,0:T(8,128)(2,1)}) %reduce-scatter.27.cloned.1.call-update) | async-done | bytes 786448 | tf_op jit(solution)/shard_map/reduce_scatter | solution.py:59
  578.7 39.4 %reduce-scatter.29.cloned.1.call-done = bf16[192,2048]{1,0:T(8,128)(2,1)} async-done(((bf16[768,2048]{1,0:T(8,128)(2,1)}), bf16[192,2048]{1,0:T(8,128)(2,1)}) %reduce-scatter.29.cloned.1.call-update) | async-done | bytes 786448 | tf_op jit(solution)/shard_map/reduce_scatter | solution.py:59
  702.5 37.5 %all-gather.23.cloned.1.call-done = bf16[768,2048]{1,0:T(8,128)(2,1)} async-done(((bf16[192,2048]{1,0:T(8,128)(2,1)}), bf16[768,2048]{1,0:T(8,128)(2,1)}) %all-gather.23.cloned.1.call-update) | async-done | bytes 3145744 | tf_op jit(solution)/shard_map/all_gather | solution.py:55
  740.0 56.9 %all-gather.45.cloned.1.call-done = bf16[1,2048,2048]{2,1,0:T(8,128)(2,1)} async-done(((bf16[1,2048,256]{2,1,0:T(8,128)(2,1)}), bf16[1,2048,2048]{2,1,0:T(8,128)(2,1)}) %all-gather.45.cloned.1.call-update) | async-done | bytes 8388624 | tf_op jit(solution)/shard_map/all_gather | solution.py:141
  822.4 60.3 %reduce-scatter.33.cloned.1.call-done = bf16[192,2048]{1,0:T(8,128)(2,1)} async-done(((bf16[768,2048]{1,0:T(8,128)(2,1)}), bf16[192,2048]{1,0:T(8,128)(2,1)}) %reduce-scatter.33.cloned.1.call-update) | async-done | bytes 786448 | tf_op jit(solution)/shard_map/reduce_scatter | solution.py:69
  888.9 63.6 %all-gather.25.cloned.1.call-done = bf16[768,2048]{1,0:T(8,128)(2,1)} async-done(((bf16[192,2048]{1,0:T(8,128)(2,1)}), bf16[768,2048]{1,0:T(8,128)(2,1)}) %all-gather.25.cloned.1.call-update) | async-done | bytes 3145744 | tf_op jit(solution)/shard_map/all_gather | solution.py:55
  958.2 44.8 %while.58 = (s32[]{:T(128)}, f32[768,128]{1,0:T(8,128)}, f32[768,128]{1,0:T(8,128)}, bf16[4,768,128]{1,2,0:T(8,128)(2,1)}, bf16[4,768,128]{2,1,0:T(8,128)(2,1)},...) while((s32[]{:T(128)}, f32[768,128]{1,0:T(8,128)}, ...), condition=%wide.region_29.31_spmd.clone, body=%wide.region_27.30_spmd.clone.sunk | while | flops 763034880 | bytes 28140772 | solution.py:253
  1031.2 58.5 %reduce-scatter.35.cloned.1.call-done = bf16[192,2048]{1,0:T(8,128)(2,1)} async-done(((bf16[768,2048]{1,0:T(8,128)(2,1)}), bf16[192,2048]{1,0:T(8,128)(2,1)}) %reduce-scatter.35.cloned.1.call-update) | async-done | bytes 786448 | tf_op jit(solution)/shard_map/reduce_scatter | solution.py:69
  1097.6 63.6 %all-gather.27.cloned.1.call-done = bf16[768,2048]{1,0:T(8,128)(2,1)} async-done(((bf16[192,2048]{1,0:T(8,128)(2,1)}), bf16[768,2048]{1,0:T(8,128)(2,1)}) %all-gather.27.cloned.1.call-update) | async-done | bytes 3145744 | tf_op jit(solution)/shard_map/all_gather | solution.py:55
  1188.6 59.0 %reduce-scatter.37.cloned.1.call-done = bf16[192,2048]{1,0:T(8,128)(2,1)} async-done(((bf16[768,2048]{1,0:T(8,128)(2,1)}), bf16[192,2048]{1,0:T(8,128)(2,1)}) %reduce-scatter.37.cloned.1.call-update) | async-done | bytes 786448 | tf_op jit(solution)/shard_map/reduce_scatter | solution.py:69
  1254.2 63.6 %all-gather.29.cloned.1.call-done = bf16[768,2048]{1,0:T(8,128)(2,1)} async-done(((bf16[192,2048]{1,0:T(8,128)(2,1)}), bf16[768,2048]{1,0:T(8,128)(2,1)}) %all-gather.29.cloned.1.call-update) | async-done | bytes 3145744 | tf_op jit(solution)/shard_map/all_gather | solution.py:55
  1323.5 40.1 %while.59 = (s32[]{:T(128)}, f32[768,128]{1,0:T(8,128)}, f32[768,128]{1,0:T(8,128)}, bf16[4,768,128]{1,2,0:T(8,128)(2,1)}, bf16[4,768,128]{2,1,0:T(8,128)(2,1)},...) while((s32[]{:T(128)}, f32[768,128]{1,0:T(8,128)}, ...), condition=%wide.region_39.41_spmd.clone, body=%wide.region_37.40_spmd.clone.sunk | while | flops 763034880 | bytes 28927240 | solution.py:253
  1493.7 77.0 %all-reduce.7.cloned.1.call-done = f32[2,8192]{1,0:T(2,128)} async-done(((f32[2,8192]{1,0:T(2,128)}), f32[2,8192]{1,0:T(2,128)}) %all-reduce.7.cloned.1.call-update) | async-done | bytes 65552 | tf_op jit(solution)/shard_map/psum | solution.py:321
  1646.4 73.4 %reduce-scatter.59.cloned.1.call-done = bf16[2048,256]{1,0:T(8,128)(2,1)} async-done(((bf16[2048,2048]{1,0:T(8,128)(2,1)}), bf16[2048,256]{1,0:T(8,128)(2,1)}) %reduce-scatter.59.cloned.1.call-update) | async-done | bytes 1048592 | tf_op jit(solution)/shard_map/reduce_scatter | solution.py:299
  1719.8 75.0 %reduce-scatter.57.cloned.1.call-done = bf16[2048,256]{1,0:T(8,128)(2,1)} async-done(((bf16[2048,2048]{1,0:T(8,128)(2,1)}), bf16[2048,256]{1,0:T(8,128)(2,1)}) %reduce-scatter.57.cloned.1.call-update) | async-done | bytes 1048592 | tf_op jit(solution)/shard_map/reduce_scatter | solution.py:299
  1798.7 58.5 %reduce-scatter.39.cloned.1.call-done = bf16[192,2048]{1,0:T(8,128)(2,1)} async-done(((bf16[768,2048]{1,0:T(8,128)(2,1)}), bf16[192,2048]{1,0:T(8,128)(2,1)}) %reduce-scatter.39.cloned.1.call-update) | async-done | bytes 786448 | tf_op jit(solution)/shard_map/reduce_scatter | solution.py:69
  1866.6 65.4 %reduce-scatter.55.cloned.1.call-done = bf16[256,2048]{1,0:T(8,128)(2,1)} async-done(((bf16[2048,2048]{1,0:T(8,128)(2,1)}), bf16[256,2048]{1,0:T(8,128)(2,1)}) %reduce-scatter.55.cloned.1.call-update) | async-done | bytes 1048592 | tf_op jit(solution)/shard_map/reduce_scatter | solution.py:296
  1932.0 75.2 %reduce-scatter.53.cloned.1.call-done = bf16[256,2048]{1,0:T(8,128)(2,1)} async-done(((bf16[2048,2048]{1,0:T(8,128)(2,1)}), bf16[256,2048]{1,0:T(8,128)(2,1)}) %reduce-scatter.53.cloned.1.call-update) | async-done | bytes 1048592 | tf_op jit(solution)/shard_map/reduce_scatter | solution.py:296
  2011.1 40.5 %reduce-scatter.51.cloned.1.call-done = bf16[512,256]{1,0:T(8,128)(2,1)} async-done(((bf16[512,2048]{1,0:T(8,128)(2,1)}), bf16[512,256]{1,0:T(8,128)(2,1)}) %reduce-scatter.51.cloned.1.call-update) | async-done | bytes 262160 | tf_op jit(solution)/shard_map/reduce_scatter | solution.py:293
  2051.6 44.9 %reduce-scatter.49.cloned.1.call-done = bf16[512,256]{1,0:T(8,128)(2,1)} async-done(((bf16[512,2048]{1,0:T(8,128)(2,1)}), bf16[512,256]{1,0:T(8,128)(2,1)}) %reduce-scatter.49.cloned.1.call-update) | async-done | bytes 262160 | tf_op jit(solution)/shard_map/reduce_scatter | solution.py:293
  2099.2 41.8 %reduce-scatter.43.cloned.1.call-done = bf16[256,512]{1,0:T(8,128)(2,1)} async-done(((bf16[2048,512]{1,0:T(8,128)(2,1)}), bf16[256,512]{1,0:T(8,128)(2,1)}) %reduce-scatter.43.cloned.1.call-update) | async-done | bytes 262160 | tf_op jit(solution)/shard_map/reduce_scatter | solution.py:287
  2141.0 44.8 %reduce-scatter.41.cloned.1.call-done = bf16[256,512]{1,0:T(8,128)(2,1)} async-done(((bf16[2048,512]{1,0:T(8,128)(2,1)}), bf16[256,512]{1,0:T(8,128)(2,1)}) %reduce-scatter.41.cloned.1.call-update) | async-done | bytes 262160 | tf_op jit(solution)/shard_map/reduce_scatter | solution.py:287
  2187.8 130.6 %all-reduce.9.cloned.1.call-done = (f32[2,2048]{1,0:T(2,128)}, f32[2,2048]{1,0:T(2,128)}, f32[2,2048]{1,0:T(2,128)}, f32[2,256]{1,0:T(2,128)}, f32[2,2048]{1,0:T...) async-done(((f32[2,2048]{1,0:T(2,128)}, f32[2,2048]{1,0:T(2,128)}, f32[2,2048]{1,0:T(2,128)}, f32[2,256]{1,0:T(2,128)}, f32[2,2048]{1,0:T(2,128)}, ...) | async-done | bytes 116752 | tf_op jit(solution)/shard_map/psum | solution.py:321
  (672 shorter events, 1044.1 us)
Async XLA Ops:
  25.0 141.6 %all-gather.33.cloned.1.call-start = ((), (), s32[]{:S(2)}) async-start(), calls=%async_computation.49 | async-start | bytes 2359296 | tf_op jit(solution)/shard_map/all_gather | solution.py:139
  44.7 188.8 %reduce-scatter.25.cloned.1.call-start = ((), (), s32[]{:S(2)}) async-start(), calls=%async_computation.25 | async-start | bytes 3932160 | tf_op jit(solution)/shard_map/reduce_scatter | solution.py:59
  175.6 172.4 %all-gather.37.cloned.1.call-start = ((), (), s32[]{:S(2)}) async-start(), calls=%async_computation.51 | async-start | bytes 9437184 | tf_op jit(solution)/shard_map/all_gather | solution.py:141
  178.6 243.4 %reduce-scatter.27.cloned.1.call-start = ((), (), s32[]{:S(2)}) async-start(), calls=%async_computation.26 | async-start | bytes 3932160 | tf_op jit(solution)/shard_map/reduce_scatter | solution.py:59
  362.4 190.1 %all-gather.41.cloned.1.call-start = ((), (), s32[]{:S(2)}) async-start(), calls=%async_computation.53 | async-start | bytes 2359296 | tf_op jit(solution)/shard_map/all_gather | solution.py:139
  460.6 157.5 %reduce-scatter.29.cloned.1.call-start = ((), (), s32[]{:S(2)}) async-start(), calls=%async_computation.27 | async-start | bytes 3932160 | tf_op jit(solution)/shard_map/reduce_scatter | solution.py:59
  558.9 181.1 %all-gather.23.cloned.1.call-start = ((), (), s32[]{:S(2)}) async-start(), calls=%async_computation.29 | async-start | bytes 3932160 | tf_op jit(solution)/shard_map/all_gather | solution.py:55
  578.1 218.8 %all-gather.45.cloned.1.call-start = ((), (), s32[]{:S(2)}) async-start(), calls=%async_computation.55 | async-start | bytes 9437184 | tf_op jit(solution)/shard_map/all_gather | solution.py:141
  578.7 304.0 %reduce-scatter.33.cloned.1.call-start = ((), (), s32[]{:S(2)}) async-start(), calls=%async_computation.30 | async-start | bytes 3932160 | tf_op jit(solution)/shard_map/reduce_scatter | solution.py:69
  1097.5 150.1 %reduce-scatter.37.cloned.1.call-start = ((), (), s32[]{:S(2)}) async-start(), calls=%async_computation.34 | async-start | bytes 3932160 | tf_op jit(solution)/shard_map/reduce_scatter | solution.py:69
  1379.9 190.8 %all-reduce.7.cloned.1.call-start = ((), (), s32[]{:S(2)}) async-start(), calls=%async_computation.45 | async-start | bytes 131072 | tf_op jit(solution)/shard_map/psum | solution.py:321
  1380.8 227.4 %reduce-scatter.47.cloned.1.call-start = ((), (), s32[]{:S(2)}) async-start(), calls=%async_computation.40 | async-start | bytes 294912 | tf_op jit(solution)/shard_map/reduce_scatter | solution.py:290
  1383.2 261.8 %reduce-scatter.45.cloned.1.call-start = ((), (), s32[]{:S(2)}) async-start(), calls=%async_computation.39 | async-start | bytes 294912 | tf_op jit(solution)/shard_map/reduce_scatter | solution.py:290
  1389.4 330.3 %reduce-scatter.59.cloned.1.call-start = ((), (), s32[]{:S(2)}) async-start(), calls=%async_computation.47 | async-start | bytes 9437184 | tf_op jit(solution)/shard_map/reduce_scatter | solution.py:299
  1404.0 390.7 %reduce-scatter.57.cloned.1.call-start = ((), (), s32[]{:S(2)}) async-start(), calls=%async_computation.46 | async-start | bytes 9437184 | tf_op jit(solution)/shard_map/reduce_scatter | solution.py:299
  1420.9 436.3 %reduce-scatter.39.cloned.1.call-start = ((), (), s32[]{:S(2)}) async-start(), calls=%async_computation.36 | async-start | bytes 3932160 | tf_op jit(solution)/shard_map/reduce_scatter | solution.py:69
  1428.2 503.8 %reduce-scatter.55.cloned.1.call-start = ((), (), s32[]{:S(2)}) async-start(), calls=%async_computation.44 | async-start | bytes 9437184 | tf_op jit(solution)/shard_map/reduce_scatter | solution.py:296
  1441.0 566.2 %reduce-scatter.53.cloned.1.call-start = ((), (), s32[]{:S(2)}) async-start(), calls=%async_computation.43 | async-start | bytes 9437184 | tf_op jit(solution)/shard_map/reduce_scatter | solution.py:296
  1454.0 597.6 %reduce-scatter.51.cloned.1.call-start = ((), (), s32[]{:S(2)}) async-start(), calls=%async_computation.42 | async-start | bytes 2359296 | tf_op jit(solution)/shard_map/reduce_scatter | solution.py:293
  1460.1 636.4 %reduce-scatter.49.cloned.1.call-start = ((), (), s32[]{:S(2)}) async-start(), calls=%async_computation.41 | async-start | bytes 2359296 | tf_op jit(solution)/shard_map/reduce_scatter | solution.py:293
  1465.2 675.8 %reduce-scatter.43.cloned.1.call-start = ((), (), s32[]{:S(2)}) async-start(), calls=%async_computation.38 | async-start | bytes 2359296 | tf_op jit(solution)/shard_map/reduce_scatter | solution.py:287
  1477.0 708.8 %reduce-scatter.41.cloned.1.call-start = ((), (), s32[]{:S(2)}) async-start(), calls=%async_computation.37 | async-start | bytes 2359296 | tf_op jit(solution)/shard_map/reduce_scatter | solution.py:287
  1862.9 458.0 %all-to-all-start.4 = ((bf16[8,24,2048]{2,1,0:T(8,128)(2,1)}), bf16[8,24,2048]{2,1,0:T(8,128)(2,1)S(1)}, u32[]{:S(2)}, u32[]{:S(2)}) async-start(bf16[8,24,2048]{2,1,0:T(8,128)(2,1)} %bitcast.336), calls=%async_computation.12 | async-start | bytes 1572864 | tf_op jit(solution)/shard_map/all_to_all | solution.py:344
  1866.5 451.9 %all-reduce.9.cloned.1.call-start = ((), (), s32[]{:S(2)}) async-start(), calls=%async_computation.58 | async-start | bytes 233472 | tf_op jit(solution)/shard_map/psum | solution.py:321
  (162 other events, 7473.7 us)
Sparse Core Ops, SparseCore 0:
  172.5 60.9 reduce-scatter.24
  235.3 54.3 all-gather.34
  292.0 55.9 all-gather.36
  361.8 60.2 reduce-scatter.26
  558.4 59.6 reduce-scatter.28
  619.9 54.4 all-gather.42
  676.4 63.4 all-gather.22
  742.3 54.5 all-gather.44
  822.5 60.2 reduce-scatter.32
  889.0 63.5 all-gather.24
  1031.3 58.4 reduce-scatter.34
  1097.6 63.5 all-gather.26
  1188.7 58.8 reduce-scatter.36
  1254.3 63.5 all-gather.28
  1388.4 58.5 reduce-scatter.30
  1453.1 117.5 all-reduce.6
  1648.4 71.2 reduce-scatter.58
  1723.5 71.2 reduce-scatter.56
  1796.9 60.2 reduce-scatter.38
  1860.6 71.3 reduce-scatter.54
  1935.9 71.2 reduce-scatter.52
  2099.7 41.2 reduce-scatter.42
  2144.5 41.2 reduce-scatter.40
  2193.4 125.0 all-reduce.8
  (10 shorter events, 306.9 us)
